TPU v7x, 256 devices: a whole 4x4x8 slice. The times are simulated.
256 devices in a mesh: row: 16 (over x_hi, z), col: 16 (over x_lo, y, core).
Axes of the slice: x: 4 (x_hi: 2, x_lo: 2; x = x_hi * 2 + x_lo), y: 4, z: 8, core: 2. Of those that a mesh axis runs over, the one named last changes fastest.
Arguments:
- log_rate: float32 [1048576], P(('row', 'col')), may hold values from -0.5 to 1
- state: float32 [1048576], P(('row', 'col')), may hold values from 0.2 to 1
- excess: float32 [1048576], P(('row', 'col')), may hold values from -0.3 to 0.3
- normal_stress: float32 [1048576], P(('row', 'col')), may hold values from 2 to 4
- rate_param: float32 [1048576], P(('row', 'col')), may hold values from 0.5 to 1
- state_param: float32 [1048576], P(('row', 'col')), may hold values from 0.5 to 1.5
- slip_length: float32 [1048576], P(('row', 'col')), may hold values from 1 to 4
- self_stiffness: float32 [1048576], P(('row', 'col')), may hold values from 0.2 to 1
- damping: float32 [1048576], P(('row', 'col')), may hold values from 1 to 2
- blocks: bfloat16 [16, 16, 512, 4096], P('row', 'col'), may hold values from -0.1796875 to 0.1796875
- pattern: int32 [16, 16, 512, 2], P('row', 'col'), may hold values from 0 to 1023
- counts: int32 [16, 16], P('row', 'col'), may hold values from 1 to 512, as said below
Outputs:
- final_log_rate: float32 [1048576], P(('row', 'col'))
- final_state: float32 [1048576], P(('row', 'col'))
- final_stress: float32 [1048576], P(('row', 'col'))
Inputs may be any that keep to these rules, and one draw needn't show every extreme that they name: `counts`: every device holds at least one live tile; some device of the first index of row holds 512.
All inputs are finite; a program needn't handle non-finite values.
Results may differ from a plain program's by a relative error of at most 0.0014.
Values may be sent and summed in bfloat16 or wider, within the bound.
No kernel may reach another device: no remote copies, remote signals or barrier semaphores. Data moves between devices by JAX's collectives and lax.ppermute only.
A program may use at most 64 MiB of HBM per device.

v0:
```python
import math
import jax
import jax.numpy as jnp
from jax import lax
from jax.sharding import PartitionSpec as P

STEPS = 2
NEWTON = 4
time_step = 0.25


def inverse_sinh(value):
    return jnp.log(value + jnp.sqrt(1.0 + value * value))


def sweep(
    kernel_tiles,
    places,
    first_slot,
    limit_slot,
    row_rates,
    col_rates,
    owner_row,
    my_col,
    per_seg,
    row_total,
    col_total,
):
    slab_length = kernel_tiles.shape[0]
    group_size = math.gcd(128, slab_length)
    row_pieces = row_rates.reshape(-1, 64)
    col_pieces = col_rates.reshape(-1, 64)

    def turn_body(turn_index, totals):
        row_acc, col_acc = totals
        begin_slot = turn_index * group_size
        block_tiles = lax.dynamic_slice_in_dim(kernel_tiles, begin_slot, group_size, 0).reshape(
            group_size, 64, 64
        )
        block_places = lax.dynamic_slice_in_dim(places, begin_slot, group_size, 0)
        row_slot = block_places[:, 0]
        col_slot = block_places[:, 1]
        slot_ids = begin_slot + jnp.arange(group_size, dtype=jnp.int32)
        active = (slot_ids >= first_slot) & (slot_ids < limit_slot)
        diagonal = (col_slot // per_seg == owner_row) & (
            row_slot == my_col * per_seg + col_slot % per_seg
        )
        direct = jnp.einsum(
            "bij,bj->bi", block_tiles, col_pieces[col_slot], preferred_element_type=jnp.float32
        )
        mirror = jnp.einsum(
            "bij,bi->bj", block_tiles, row_pieces[row_slot], preferred_element_type=jnp.float32
        )
        direct = jnp.where(active[:, None], direct, 0.0)
        mirror = jnp.where((active & jnp.logical_not(diagonal))[:, None], mirror, 0.0)
        return (row_acc.at[row_slot].add(direct), col_acc.at[col_slot].add(mirror))

    lower = jnp.maximum(first_slot, 0) // group_size
    upper = (jnp.maximum(limit_slot, 0) + group_size - 1) // group_size
    upper = jnp.maximum(upper, lower)
    return lax.fori_loop(lower, upper, turn_body, (row_total, col_total))


def friction_solve(rate_log, stress, state, normal_stress, rate_param, damping):
    for turn_index in range(NEWTON):
        speed = jnp.exp(rate_log)
        ratio = 0.5 * jnp.exp(rate_log + state / rate_param)
        misfit = stress - damping * speed - normal_stress * rate_param * inverse_sinh(ratio)
        slope = -damping * speed - normal_stress * rate_param * ratio / jnp.sqrt(
            1.0 + ratio * ratio
        )
        rate_log = rate_log - misfit / slope
    return rate_log


def on_device(
    log_rate,
    state,
    excess,
    normal_stress,
    rate_param,
    state_param,
    slip_length,
    self_stiffness,
    damping,
    blocks,
    pattern,
    counts,
):
    patches = log_rate.shape[0]
    per_seg = patches // 64
    my_row = lax.axis_index("row")
    my_col = lax.axis_index("col")
    row_count = lax.axis_size("row")
    col_count = lax.axis_size("col")
    kernel_tiles = blocks.reshape(blocks.shape[2], blocks.shape[3])
    places = pattern.reshape(pattern.shape[2], 2)
    stored = counts[0, 0]
    rate_log = log_rate
    balance = normal_stress * rate_param * inverse_sinh(
        0.5 * jnp.exp(log_rate + state / rate_param)
    ) + damping * jnp.exp(log_rate)
    stress = balance * (1.0 + excess)
    for step_index in range(STEPS):
        speed = jnp.exp(rate_log)
        pushed = (speed - 1.0).astype(jnp.bfloat16)
        row_rates = lax.all_gather(pushed, "col", axis=0, tiled=True)
        col_rates = lax.all_gather(pushed, "row", axis=0, tiled=True)
        row_total = jnp.zeros((col_count * per_seg, 64), jnp.float32)
        col_total = jnp.zeros((row_count * per_seg, 64), jnp.float32)
        row_total, col_total = sweep(
            kernel_tiles,
            places,
            0,
            stored,
            row_rates,
            col_rates,
            my_row,
            my_col,
            per_seg,
            row_total,
            col_total,
        )
        stress_rate = lax.psum_scatter(
            row_total.reshape(-1).astype(jnp.bfloat16), "col", scatter_dimension=0, tiled=True
        ).astype(jnp.float32) + lax.psum_scatter(
            col_total.reshape(-1).astype(jnp.bfloat16), "row", scatter_dimension=0, tiled=True
        ).astype(
            jnp.float32
        )
        new_stress = stress + time_step * (stress_rate - self_stiffness * (speed - 1.0))
        state = state + time_step * (state_param / slip_length) * (
            jnp.exp(-state / state_param) - speed
        )
        stress = new_stress
        rate_log = friction_solve(rate_log, stress, state, normal_stress, rate_param, damping)
    return (rate_log, state, stress)


def solution(mesh):
    in_specs = (
        P(("row", "col")),
        P(("row", "col")),
        P(("row", "col")),
        P(("row", "col")),
        P(("row", "col")),
        P(("row", "col")),
        P(("row", "col")),
        P(("row", "col")),
        P(("row", "col")),
        P("row", "col", None, None),
        P("row", "col", None, None),
        P("row", "col"),
    )
    out_specs = (P(("row", "col")), P(("row", "col")), P(("row", "col")))
    return jax.shard_map(
        on_device, mesh=mesh, in_specs=in_specs, out_specs=out_specs, check_vma=False
    )
```

profile of v0, /device:TPU:1, one launch (start us, length us, event | category | flops | bytes accessed | tf_op | source)
XLA Modules:
  0.0 812.9 jit_solution(1112874415453995245)
XLA Ops:
  8.6 38.1 %all_gather.12 = bf16[65536]{0:T(1024)(128)(2,1)S(1)} all-gather(bf16[4096]{0:T(1024)(128)(2,1)S(1)} %add_convert_fusion), channel_id=1, replica_groups=mesh['row'=16,'col'=16] {'row'}, dimensions={0}, use_global_device_ids=true | all-gather | bytes 139264 | tf_op jit(solution)/shard_map/all_gather | solution.py:108
  46.7 27.0 %all_gather.13 = bf16[65536]{0:T(1024)(128)(2,1)S(1)} all-gather(bf16[4096]{0:T(1024)(128)(2,1)S(1)} %add_convert_fusion), channel_id=1, replica_groups=mesh['row'=16,'col'=16] {'col'}, dimensions={0}, use_global_device_ids=true | all-gather | bytes 139264 | tf_op jit(solution)/shard_map/all_gather | solution.py:107
  73.7 6.5 copy.16
  82.9 42.3 %while.28 = (s32[]{:T(128)}, f32[1024,64]{1,0:T(8,128)}, f32[1024,64]{1,0:T(8,128)}, s32[]{:T(128)}, s32[512,2]{0,1:T(2,128)S(1)}, /*index=5*/s32[]{:T(128)}, bf...) while((s32[]{:T(128)}, f32[1024,64]{1,0:T(8,128)}, ...), condition=%wide.region_3.4_spmd, body=%wide.region_0.3_spmd.sunk | while | flops 2136966 | bytes 9749571 | solution.py:61
  84.2 3.5 copy.45
  89.8 1.5 scatter_custom_fusion.18
  93.9 3.1 scatter_custom_fusion.19
  98.3 3.5 copy.45
  108.0 3.1 scatter_custom_fusion.19
  112.4 3.5 copy.45
  122.1 3.1 scatter_custom_fusion.19
  131.8 147.2 %all-reduce.11.cloned.1.call-done = bf16[65536]{0:T(1024)(128)(2,1)} async-done(((bf16[65536]{0:T(1024)(128)(2,1)}), bf16[65536]{0:T(1024)(128)(2,1)}) %all-reduce.11.cloned.1.call-update) | async-done | bytes 131088
  278.9 133.4 %all-reduce.9.cloned.1.call-done = bf16[65536]{0:T(1024)(128)(2,1)} async-done(((bf16[65536]{0:T(1024)(128)(2,1)}), bf16[65536]{0:T(1024)(128)(2,1)}) %all-reduce.9.cloned.1.call-update) | async-done | bytes 131088
  413.9 34.4 %all_gather.14 = bf16[65536]{0:T(1024)(128)(2,1)S(1)} all-gather(bf16[4096]{0:T(1024)(128)(2,1)S(1)} %get-tuple-element.346), channel_id=1, replica_groups=mesh['row'=16,'col'=16] {'row'}, dimensions={0}, use_global_device_ids=true | all-gather | bytes 139264 | tf_op jit(solution)/shard_map/all_gather | solution.py:108
  448.3 24.1 %all_gather.15 = bf16[65536]{0:T(1024)(128)(2,1)S(1)} all-gather(bf16[4096]{0:T(1024)(128)(2,1)S(1)} %get-tuple-element.346), channel_id=1, replica_groups=mesh['row'=16,'col'=16] {'col'}, dimensions={0}, use_global_device_ids=true | all-gather | bytes 139264 | tf_op jit(solution)/shard_map/all_gather | solution.py:107
  475.0 42.3 %while.29 = (s32[]{:T(128)}, f32[1024,64]{1,0:T(8,128)}, f32[1024,64]{1,0:T(8,128)}, s32[]{:T(128)}, s32[512,2]{0,1:T(2,128)S(1)}, /*index=5*/s32[]{:T(128)}, bf...) while((s32[]{:T(128)}, f32[1024,64]{1,0:T(8,128)}, ...), condition=%wide.region_9.10_spmd, body=%wide.region_6.9_spmd.sunk | while | flops 2136966 | bytes 9749571 | solution.py:61
  476.3 3.5 copy.48
  486.0 3.1 scatter_custom_fusion.23
  490.4 3.5 copy.48
  500.1 3.1 scatter_custom_fusion.23
  504.5 3.5 copy.48
  514.2 3.1 scatter_custom_fusion.23
  521.2 150.4 %all-reduce.15.cloned.1.call-done = bf16[65536]{0:T(1024)(128)(2,1)} async-done(((bf16[65536]{0:T(1024)(128)(2,1)}), bf16[65536]{0:T(1024)(128)(2,1)}) %all-reduce.15.cloned.1.call-update) | async-done | bytes 131088
  671.6 133.2 %all-reduce.13.cloned.1.call-done = bf16[65536]{0:T(1024)(128)(2,1)} async-done(((bf16[65536]{0:T(1024)(128)(2,1)}), bf16[65536]{0:T(1024)(128)(2,1)}) %all-reduce.13.cloned.1.call-update) | async-done | bytes 131088
  (158 shorter events, 61.3 us)
Async XLA Ops:
  7.2 271.8 %all-reduce.11.cloned.1.call-start = ((), (), s32[]{:S(2)}) async-start(), calls=%async_computation.1 | async-start | bytes 262144
  73.7 9.2 %copy-start.16 = (s32[1,1,512,2]{2,3,1,0:T(2,128)S(1)}, s32[1,1,512,2]{2,3,1,0:T(2,128)}, u32[]{:S(2)}) copy-start(s32[1,1,512,2]{2,3,1,0:T(2,128)} %param.26) | copy-start | bytes 12292
  91.3 5.7 copy-start.3
  105.4 5.7 copy-start.3
  119.5 5.7 copy-start.3
  125.2 4.1 copy-start.19
  125.2 4.7 copy-start.18
  125.2 287.1 %copy-start.6 = (f32[4096]{0:T(1024)S(1)}, f32[4096]{0:T(1024)}, u32[]{:S(2)}) copy-start(f32[4096]{0:T(1024)} %param.16) | copy-start | bytes 49156
  125.2 287.1 %copy-start.7 = (f32[4096]{0:T(1024)S(1)}, f32[4096]{0:T(1024)}, u32[]{:S(2)}) copy-start(f32[4096]{0:T(1024)} %param.24) | copy-start | bytes 49156
  125.2 287.1 %copy-start.8 = (f32[4096]{0:T(1024)S(1)}, f32[4096]{0:T(1024)}, u32[]{:S(2)}) copy-start(f32[4096]{0:T(1024)} %param.20) | copy-start | bytes 49156
  125.2 287.1 %copy-start.9 = (f32[4096]{0:T(1024)S(1)}, f32[4096]{0:T(1024)}, u32[]{:S(2)}) copy-start(f32[4096]{0:T(1024)} %param.17) | copy-start | bytes 49156
  125.2 287.1 %copy-start.10 = (f32[4096]{0:T(1024)S(1)}, f32[4096]{0:T(1024)}, u32[]{:S(2)}) copy-start(f32[4096]{0:T(1024)} %param.21) | copy-start | bytes 49156
  125.3 287.1 %copy-start.11 = (f32[4096]{0:T(1024)S(1)}, f32[4096]{0:T(1024)}, u32[]{:S(2)}) copy-start(f32[4096]{0:T(1024)} %param.22) | copy-start | bytes 49156
  125.3 287.1 %copy-start.12 = (f32[4096]{0:T(1024)S(1)}, f32[4096]{0:T(1024)}, u32[]{:S(2)}) copy-start(f32[4096]{0:T(1024)} %param.23) | copy-start | bytes 49156
  125.3 287.1 %copy-start.13 = (f32[4096]{0:T(1024)S(1)}, f32[4096]{0:T(1024)}, u32[]{:S(2)}) copy-start(f32[4096]{0:T(1024)} %param.18) | copy-start | bytes 49156
  125.3 287.1 %copy-start.17 = (f32[4096]{0:T(1024)S(1)}, f32[4096]{0:T(1024)}, u32[]{:S(2)}) copy-start(f32[4096]{0:T(1024)} %param.19) | copy-start | bytes 49156
  127.3 285.0 %all-reduce.9.cloned.1.call-start = ((), (), s32[]{:S(2)}) async-start(), calls=%async_computation | async-start | bytes 262144
  129.2 542.3 %all-reduce.15.cloned.1.call-start = ((), (), s32[]{:S(2)}) async-start(), calls=%async_computation.3 | async-start | bytes 262144
  483.5 5.7 copy-start.5
  497.6 5.7 copy-start.5
  511.7 5.7 copy-start.5
  517.3 287.5 %copy-start.14 = (f32[4096]{0:T(1024)S(1)}, f32[4096]{0:T(1024)}, u32[]{:S(2)}) copy-start(f32[4096]{0:T(1024)} %get-tuple-element.347) | copy-start | bytes 49156
  517.3 287.5 %copy-start.15 = (f32[4096]{0:T(1024)S(1)}, f32[4096]{0:T(1024)}, u32[]{:S(2)}) copy-start(f32[4096]{0:T(1024)} %get-tuple-element.348) | copy-start | bytes 49156
  519.2 285.6 %all-reduce.13.cloned.1.call-start = ((), (), s32[]{:S(2)}) async-start(), calls=%async_computation.2 | async-start | bytes 262144
  (12 other events, 34.1 us)
Sparse Core Ops, SparseCore 0:
  127.4 151.4 all-reduce.10
  281.5 130.7 all-reduce.8
  519.4 152.1 all-reduce.14
  674.0 130.7 all-reduce.12
where the time goes:
time: 814 us; the launch traced here: 813 us
  waiting for transfers between devices  564 us (69%)
  blocking collectives  124 us (15%)
  local copies, waits for them, and re-layouts  53.7 us (7%)
  other arithmetic  43.9 us (5%)
  between operations  15.9 us (2%)
  matrix products  10.9 us (1%)
    unnamed x8, waiting for transfers between devices  564 us
    all_gather x2, blocking collectives, on_device(): col_rates = lax.all_gather(pushed, 'row', axis=0, tiled=True)  72.5 us
    all_gather x2, blocking collectives, on_device(): row_rates = lax.all_gather(pushed, 'col', axis=0, tiled=True)  51.1 us
    scatter-add x12, other arithmetic, turn_body(): return (row_acc.at[row_slot].add(direct), col_acc.at[col_slot].add(mirror))  27.6 us
    reshape x6, local copies, waits for them, and re-layouts, turn_body(): lax.dynamic_slice_in_dim(kernel_tiles, begin_slot, group_size, 0)  21 us
  transfers between devices with their start and end apart: 4, of which 4 were waited for; matrix products, arithmetic and copies ran while one was open for 1% of the time, Pallas kernels for 0%

commit v1 on v0

--- a/solution.py
+++ b/solution.py
@@ -105,7 +105,10 @@
         speed = jnp.exp(rate_log)
         pushed = (speed - 1.0).astype(jnp.bfloat16)
         row_rates = lax.all_gather(pushed, "col", axis=0, tiled=True)
-        col_rates = lax.all_gather(pushed, "row", axis=0, tiled=True)
+        n_dev = lax.axis_size("row")
+        pieces = jnp.stack([pushed for _ in range(n_dev)])
+        pieces = lax.all_to_all(pieces, "row", split_axis=0, concat_axis=0)
+        col_rates = jnp.concatenate(pieces, axis=0)
         row_total = jnp.zeros((col_count * per_seg, 64), jnp.float32)
         col_total = jnp.zeros((row_count * per_seg, 64), jnp.float32)
         row_total, col_total = sweep(

time: 814 us -> 764 us (0.939)
  blocking collectives: 124 us -> 37.4 us
  starting transfers between devices: 0.16 us -> 20.7 us
  local copies, waits for them, and re-layouts: 53.7 us -> 67.1 us
    all_gather x2 -> x0, blocking collectives: 72.5 us -> none  [on_device(): col_rates = lax.all_gather(pushed, 'row', axis=0, tiled=True)]
    all_to_all x0 -> x2, starting transfers between devices: none -> 20.5 us  [on_device(): pieces = lax.all_to_all(pieces, 'row', split_axis=0, concat_axis=0)]
    all_gather x2, blocking collectives: 51.1 us -> 37.4 us  [on_device(): row_rates = lax.all_gather(pushed, 'col', axis=0, tiled=True)]
    scatter-add x12, other arithmetic: 27.6 us -> 18.5 us  [turn_body(): return (row_acc.at[row_slot].add(direct), col_acc.at[col_slot].add(mirror))]
  transfers between devices with their start and end apart: 4 -> 6, of which waited for: 4 -> 4; matrix products, arithmetic and copies ran while one was open for 1% -> 2% of each run, Pallas kernels for 0% -> 0%
where the time goes in v1:
time: 764 us; the launch traced here: 763 us
  waiting for transfers between devices  571 us (75%)
  local copies, waits for them, and re-layouts  67.1 us (9%)
  other arithmetic  39.2 us (5%)
  blocking collectives  37.4 us (5%)
  starting transfers between devices  20.7 us (3%)
  between operations  16.1 us (2%)
  matrix products  10.9 us (1%)
    unnamed x8, waiting for transfers between devices  571 us
    all_gather x2, blocking collectives, on_device(): row_rates = lax.all_gather(pushed, 'col', axis=0, tiled=True)  37.4 us
    reshape x6, local copies, waits for them, and re-layouts, turn_body(): lax.dynamic_slice_in_dim(kernel_tiles, begin_slot, group_size, 0)  21 us
    all_to_all x2, starting transfers between devices, on_device(): pieces = lax.all_to_all(pieces, 'row', split_axis=0, concat_axis=0)  20.5 us
    scatter-add x12, other arithmetic, turn_body(): return (row_acc.at[row_slot].add(direct), col_acc.at[col_slot].add(mirror))  18.5 us
  transfers between devices with their start and end apart: 6, of which 4 were waited for; matrix products, arithmetic and copies ran while one was open for 2% of the time, Pallas kernels for 0%

profile of v1, /device:TPU:1, one launch (start us, length us, event | category | flops | bytes accessed | tf_op | source)
XLA Modules:
  0.0 762.6 jit_solution(7761970742180390504)
XLA Ops:
  10.6 11.6 %all-to-all-start = ((bf16[16,2,2048]{2,1,0:T(2,128)(2,1)}), bf16[16,2,2048]{2,1,0:T(2,128)(2,1)S(1)}, u32[]{:S(2)}, u32[]{:S(2)}) async-start(bf16[16,2,2048]{2,1,0:T(2,128)(2,1)} %reshape.180), calls=%async_computation | async-start | bytes 262144 | tf_op jit(solution)/shard_map/all_to_all | solution.py:110
  22.9 6.5 copy.16
  29.4 20.2 %all_gather.6 = bf16[65536]{0:T(1024)(128)(2,1)S(1)} all-gather(bf16[4096]{0:T(1024)(128)(2,1)S(1)} %add_convert_fusion), channel_id=1, replica_groups=mesh['row'=16,'col'=16] {'col'}, dimensions={0}, use_global_device_ids=true | all-gather | bytes 139264 | tf_op jit(solution)/shard_map/all_gather | solution.py:107
  53.3 43.2 %while.28 = (s32[]{:T(128)}, f32[1024,64]{1,0:T(8,128)}, f32[1024,64]{1,0:T(8,128)}, s32[]{:T(128)}, s32[512,2]{0,1:T(2,128)S(1)}, /*index=5*/s32[]{:T(128)}, bf...) while((s32[]{:T(128)}, f32[1024,64]{1,0:T(8,128)}, ...), condition=%wide.region_3.4_spmd, body=%wide.region_0.3_spmd.sunk | while | flops 2136966 | bytes 11321955 | solution.py:61
  54.6 3.5 copy.45
  58.2 1.7 gather_fusion
  69.0 3.5 copy.45
  72.6 1.7 gather_fusion
  83.4 3.5 copy.45
  87.0 1.7 gather_fusion
  103.0 150.2 %all-reduce.11.cloned.1.call-done = bf16[65536]{0:T(1024)(128)(2,1)} async-done(((bf16[65536]{0:T(1024)(128)(2,1)}), bf16[65536]{0:T(1024)(128)(2,1)}) %all-reduce.11.cloned.1.call-update) | async-done | bytes 131088
  253.2 133.4 %all-reduce.9.cloned.1.call-done = bf16[65536]{0:T(1024)(128)(2,1)} async-done(((bf16[65536]{0:T(1024)(128)(2,1)}), bf16[65536]{0:T(1024)(128)(2,1)}) %all-reduce.9.cloned.1.call-update) | async-done | bytes 131088
  390.4 9.0 %all-to-all-start.1 = ((bf16[16,2,2048]{2,1,0:T(2,128)(2,1)}), bf16[16,2,2048]{2,1,0:T(2,128)(2,1)S(1)}, u32[]{:S(2)}, u32[]{:S(2)}) async-start(bf16[16,2,2048]{2,1,0:T(2,128)(2,1)} %reshape.182), calls=%async_computation.1 | async-start | bytes 262144 | tf_op jit(solution)/shard_map/all_to_all | solution.py:110
  399.4 17.1 %all_gather.7 = bf16[65536]{0:T(1024)(128)(2,1)S(1)} all-gather(bf16[4096]{0:T(1024)(128)(2,1)S(1)} %get-tuple-element.346), channel_id=1, replica_groups=mesh['row'=16,'col'=16] {'col'}, dimensions={0}, use_global_device_ids=true | all-gather | bytes 139264 | tf_op jit(solution)/shard_map/all_gather | solution.py:107
  420.2 43.2 %while.29 = (s32[]{:T(128)}, f32[1024,64]{1,0:T(8,128)}, f32[1024,64]{1,0:T(8,128)}, s32[]{:T(128)}, s32[512,2]{0,1:T(2,128)S(1)}, /*index=5*/s32[]{:T(128)}, bf...) while((s32[]{:T(128)}, f32[1024,64]{1,0:T(8,128)}, ...), condition=%wide.region_9.10_spmd, body=%wide.region_6.9_spmd.sunk | while | flops 2136966 | bytes 11321955 | solution.py:61
  421.5 3.5 copy.48
  425.1 1.7 gather_fusion.2
  435.9 3.5 copy.48
  439.5 1.7 gather_fusion.2
  450.4 3.5 copy.48
  453.9 1.7 gather_fusion.2
  467.4 153.8 %all-reduce.15.cloned.1.call-done = bf16[65536]{0:T(1024)(128)(2,1)} async-done(((bf16[65536]{0:T(1024)(128)(2,1)}), bf16[65536]{0:T(1024)(128)(2,1)}) %all-reduce.15.cloned.1.call-update) | async-done | bytes 131088
  621.3 133.2 %all-reduce.13.cloned.1.call-done = bf16[65536]{0:T(1024)(128)(2,1)} async-done(((bf16[65536]{0:T(1024)(128)(2,1)}), bf16[65536]{0:T(1024)(128)(2,1)}) %all-reduce.13.cloned.1.call-update) | async-done | bytes 131088
  754.5 1.5 divide_subtract_fusion
  (195 shorter events, 78.3 us)
Async XLA Ops:
  10.6 39.2 %all-to-all-start = ((bf16[16,2,2048]{2,1,0:T(2,128)(2,1)}), bf16[16,2,2048]{2,1,0:T(2,128)(2,1)S(1)}, u32[]{:S(2)}, u32[]{:S(2)}) async-start(bf16[16,2,2048]{2,1,0:T(2,128)(2,1)} %reshape.180), calls=%async_computation | async-start | bytes 262144 | tf_op jit(solution)/shard_map/all_to_all | solution.py:110
  22.2 231.0 %all-reduce.11.cloned.1.call-start = ((), (), s32[]{:S(2)}) async-start(), calls=%async_computation.3 | async-start | bytes 262144
  29.4 23.9 %copy-start.24 = (s32[1,1,512,2]{2,3,1,0:T(2,128)S(1)}, s32[1,1,512,2]{2,3,1,0:T(2,128)}, u32[]{:S(2)}) copy-start(s32[1,1,512,2]{2,3,1,0:T(2,128)} %param.26) | copy-start | bytes 12292
  96.5 290.1 %copy-start.8 = (f32[4096]{0:T(1024)S(1)}, f32[4096]{0:T(1024)}, u32[]{:S(2)}) copy-start(f32[4096]{0:T(1024)} %param.16) | copy-start | bytes 49156
  96.5 290.1 %copy-start.9 = (f32[4096]{0:T(1024)S(1)}, f32[4096]{0:T(1024)}, u32[]{:S(2)}) copy-start(f32[4096]{0:T(1024)} %param.24) | copy-start | bytes 49156
  96.5 290.1 %copy-start.10 = (f32[4096]{0:T(1024)S(1)}, f32[4096]{0:T(1024)}, u32[]{:S(2)}) copy-start(f32[4096]{0:T(1024)} %param.20) | copy-start | bytes 49156
  96.6 290.1 %copy-start.12 = (f32[4096]{0:T(1024)S(1)}, f32[4096]{0:T(1024)}, u32[]{:S(2)}) copy-start(f32[4096]{0:T(1024)} %param.17) | copy-start | bytes 49156
  96.6 290.1 %copy-start.14 = (f32[4096]{0:T(1024)S(1)}, f32[4096]{0:T(1024)}, u32[]{:S(2)}) copy-start(f32[4096]{0:T(1024)} %param.21) | copy-start | bytes 49156
  96.6 290.1 %copy-start.16 = (f32[4096]{0:T(1024)S(1)}, f32[4096]{0:T(1024)}, u32[]{:S(2)}) copy-start(f32[4096]{0:T(1024)} %param.22) | copy-start | bytes 49156
  96.6 290.1 %copy-start.18 = (f32[4096]{0:T(1024)S(1)}, f32[4096]{0:T(1024)}, u32[]{:S(2)}) copy-start(f32[4096]{0:T(1024)} %param.23) | copy-start | bytes 49156
  96.6 290.0 %copy-start.20 = (f32[4096]{0:T(1024)S(1)}, f32[4096]{0:T(1024)}, u32[]{:S(2)}) copy-start(f32[4096]{0:T(1024)} %param.18) | copy-start | bytes 49156
  96.6 290.0 %copy-start.25 = (f32[4096]{0:T(1024)S(1)}, f32[4096]{0:T(1024)}, u32[]{:S(2)}) copy-start(f32[4096]{0:T(1024)} %param.19) | copy-start | bytes 49156
  98.6 288.0 %all-reduce.9.cloned.1.call-start = ((), (), s32[]{:S(2)}) async-start(), calls=%async_computation.2 | async-start | bytes 262144
  390.4 26.3 %all-to-all-start.1 = ((bf16[16,2,2048]{2,1,0:T(2,128)(2,1)}), bf16[16,2,2048]{2,1,0:T(2,128)(2,1)S(1)}, u32[]{:S(2)}, u32[]{:S(2)}) async-start(bf16[16,2,2048]{2,1,0:T(2,128)(2,1)} %reshape.182), calls=%async_computation.1 | async-start | bytes 262144 | tf_op jit(solution)/shard_map/all_to_all | solution.py:110
  399.4 221.9 %all-reduce.15.cloned.1.call-start = ((), (), s32[]{:S(2)}) async-start(), calls=%async_computation.5 | async-start | bytes 262144
  463.5 291.0 %copy-start.11 = (f32[4096]{0:T(1024)S(1)}, f32[4096]{0:T(1024)}, u32[]{:S(2)}) copy-start(f32[4096]{0:T(1024)} %param.20) | copy-start | bytes 49156
  463.5 291.0 %copy-start.13 = (f32[4096]{0:T(1024)S(1)}, f32[4096]{0:T(1024)}, u32[]{:S(2)}) copy-start(f32[4096]{0:T(1024)} %param.17) | copy-start | bytes 49156
  463.5 291.0 %copy-start.15 = (f32[4096]{0:T(1024)S(1)}, f32[4096]{0:T(1024)}, u32[]{:S(2)}) copy-start(f32[4096]{0:T(1024)} %param.21) | copy-start | bytes 49156
  463.5 291.0 %copy-start.17 = (f32[4096]{0:T(1024)S(1)}, f32[4096]{0:T(1024)}, u32[]{:S(2)}) copy-start(f32[4096]{0:T(1024)} %param.22) | copy-start | bytes 49156
  463.5 291.0 %copy-start.19 = (f32[4096]{0:T(1024)S(1)}, f32[4096]{0:T(1024)}, u32[]{:S(2)}) copy-start(f32[4096]{0:T(1024)} %param.23) | copy-start | bytes 49156
  463.5 291.0 %copy-start.21 = (f32[4096]{0:T(1024)S(1)}, f32[4096]{0:T(1024)}, u32[]{:S(2)}) copy-start(f32[4096]{0:T(1024)} %param.18) | copy-start | bytes 49156
  463.5 291.0 %copy-start.22 = (f32[4096]{0:T(1024)S(1)}, f32[4096]{0:T(1024)}, u32[]{:S(2)}) copy-start(f32[4096]{0:T(1024)} %get-tuple-element.347) | copy-start | bytes 49156
  463.5 291.0 %copy-start.23 = (f32[4096]{0:T(1024)S(1)}, f32[4096]{0:T(1024)}, u32[]{:S(2)}) copy-start(f32[4096]{0:T(1024)} %get-tuple-element.348) | copy-start | bytes 49156
  465.5 289.0 %all-reduce.13.cloned.1.call-start = ((), (), s32[]{:S(2)}) async-start(), calls=%async_computation.4 | async-start | bytes 262144
  (26 other events, 86.2 us)
Sparse Core Ops, SparseCore 0:
  98.7 154.4 all-reduce.10
  255.8 130.7 all-reduce.8
  465.6 155.6 all-reduce.14
  623.7 130.7 all-reduce.12
